TPU v7x, 32 devices: a whole 2x2x4 slice. The times are simulated.
32 devices in a mesh: row: 4 (over z), replica: 4 (over y, core), feat: 2 (over x).
Axes of the slice: x: 2, y: 2, z: 4, core: 2. Of those that a mesh axis runs over, the one named last changes fastest.
Arguments:
- features: bfloat16 [4, 4096, 256], P('replica', ('row', 'feat')), may hold values from -6 to 6
- tiles: bfloat16 [4, 32, 4, 3, 128, 128], P('replica', ('row', 'feat')), may hold values from 0 to 1
- block_cols: int32 [4, 32, 4, 3], P('replica', ('row', 'feat')), may hold values from 0 to 7
- block_counts: int32 [4, 32, 4], P('replica', ('row', 'feat')), may hold values from 0 to 3, as said below
- degrees: int32 [4, 4096], P('replica', ('row', 'feat')), may hold values from 32 to 287
- w_self: bfloat16 [256, 256], P(None, 'feat'), may hold values from -0.375 to 0.375
- w_neigh: bfloat16 [256, 256], P(None, 'feat'), may hold values from -0.375 to 0.375
- gamma: float32 [256], P('feat'), may hold values from 0.5 to 1.5
- beta: float32 [256], P('feat'), may hold values from -3 to 3
Outputs:
- hidden_out: bfloat16 [4, 4096, 256], P('replica', 'row', 'feat')
Inputs may be any that keep to these rules, and one draw needn't show every extreme that they name: `block_counts`: some block row uses all 3 slots of some source shard in every partition.
All inputs are finite; a program needn't handle non-finite values.
Results may differ from a plain program's by a relative error of at most 0.001.
Values may be sent and summed in bfloat16 or wider, within the bound.
No kernel may reach another device: no remote copies, remote signals or barrier semaphores. Data moves between devices by JAX's collectives and lax.ppermute only.
A program may use at most 128 MiB of HBM per device.

v0:
```python
import jax
import jax.numpy as jnp
from jax import lax
from jax.sharding import PartitionSpec as P


def per_device(features, tiles, block_cols, block_counts, degrees, w_self, w_neigh, gamma, beta):
    local_x = features[0]
    local_tiles = tiles[0]
    local_cols = block_cols[0]
    local_counts = block_counts[0]
    nodes_here = local_x.shape[0]
    width = local_x.shape[1]
    block_size = local_tiles.shape[3]
    slots = local_tiles.shape[2]
    row_blocks = local_tiles.shape[0]
    pair = lax.all_gather(local_x, "feat", axis=0, tiled=True)
    shard_rows = pair.shape[0]
    shard_blocks = shard_rows // block_size
    slot_index = jnp.arange(slots, dtype=jnp.int32)[None, :]
    start_total = jnp.zeros((row_blocks, block_size, width), jnp.float32)
    piece = lax.all_gather(pair, "row", axis=0, tiled=True)
    count_shards = piece.shape[0] // shard_rows
    shards = piece.reshape(count_shards, shard_blocks, block_size, width)

    def one_shard(step, acc):
        shard = lax.dynamic_index_in_dim(shards, step, 0, keepdims=False)
        counts_now = lax.dynamic_index_in_dim(local_counts, step, 1, keepdims=False)
        cols_now = lax.dynamic_index_in_dim(local_cols, step, 1, keepdims=False)
        tiles_now = lax.dynamic_index_in_dim(local_tiles, step, 1, keepdims=False)
        picked = shard[cols_now]
        used = slot_index < counts_now[:, None]
        masked = jnp.where(used[:, :, None, None], tiles_now, jnp.zeros((), tiles_now.dtype))
        return acc + jnp.einsum(
            "bcij,bcjf->bif", masked, picked, preferred_element_type=jnp.float32
        )

    agg_sum = lax.fori_loop(0, count_shards, one_shard, start_total).reshape(nodes_here, width)
    agg = (agg_sum / degrees[0][:, None].astype(jnp.float32)).astype(jnp.bfloat16)
    agg_pair = lax.all_gather(agg, "feat", axis=0, tiled=True)
    pre = jnp.dot(pair, w_self, preferred_element_type=jnp.float32) + jnp.dot(
        agg_pair, w_neigh, preferred_element_type=jnp.float32
    )
    col_sum, col_sq = lax.psum(
        (jnp.sum(pre, axis=0), jnp.sum(pre * pre, axis=0)), ("row", "replica")
    )
    total_nodes = pre.shape[0] * lax.axis_size("row") * lax.axis_size("replica")
    mean = col_sum / total_nodes
    var = col_sq / total_nodes - mean * mean
    normed = gamma * (pre - mean) / jnp.sqrt(var + 1e-05) + beta
    return jnp.maximum(normed, 0.0).astype(jnp.bfloat16)[None]


def solution(mesh):
    in_specs = (
        P("replica", ("row", "feat"), None),
        P("replica", ("row", "feat"), None, None, None, None),
        P("replica", ("row", "feat"), None, None),
        P("replica", ("row", "feat"), None),
        P("replica", ("row", "feat")),
        P(None, "feat"),
        P(None, "feat"),
        P("feat"),
        P("feat"),
    )
    out_specs = P("replica", "row", "feat")
    return jax.shard_map(
        per_device, mesh=mesh, in_specs=in_specs, out_specs=out_specs, check_vma=False
    )
```

profile of v0, /device:TPU:0, one launch (start us, length us, event | category | flops | bytes accessed | tf_op | source)
XLA Modules:
  0.0 121.8 jit_solution(17375432722191585981)
XLA Ops:
  6.5 12.0 %all-gather = bf16[1,1024,256]{2,1,0:T(8,128)(2,1)} all-gather(bf16[1,512,256]{2,1,0:T(8,128)(2,1)} %param.11), channel_id=2, replica_groups=mesh['row'=4,'replica'=4,'feat'=2] {'feat'}, dimensions={1}, use_global_device_ids=true | all-gather | bytes 786432 | tf_op jit(solution)/shard_map/all_gather | solution.py:17
  18.7 1.6 %copy.20 = bf16[1,4,4,3,128,128]{5,4,3,1,2,0:T(8,128)(2,1)S(1)} copy(bf16[1,4,4,3,128,128]{5,4,3,2,1,0:T(8,128)(2,1)} %param.12) | data formatting | bytes 3145728 | tf_op args[1]
  20.3 0.1 copy.17
  20.5 1.1 fusion.10
  21.6 43.2 %all-gather.4.cloned.1.call-done = bf16[1,4096,256]{2,1,0:T(8,128)(2,1)} async-done(((bf16[1,1024,256]{2,1,0:T(8,128)(2,1)}), bf16[1,4096,256]{2,1,0:T(8,128)(2,1)}) %all-gather.4.cloned.1.call-update) | async-done | bytes 2097168 | tf_op jit(solution)/shard_map/all_gather | solution.py:22
  64.7 9.8 %while.14 = (s32[]{:T(128)}, f32[4,128,256]{2,1,0:T(8,128)S(1)}, s32[4,4]{0,1:T(4,128)S(1)}, bf16[4,4,3,128,128]{4,3,2,0,1:T(8,128)(2,1)S(1)}, bf16[4,8,128,256]...) while((s32[]{:T(128)}, f32[4,128,256]{2,1,0:T(8,128)S(1)}, ...), condition=%wide.region_1.2_spmd.clone, body=%wide.region_0.1_spmd.clone.sunk | while | flops 101123120 | bytes 4854827 | solution.py:38
  64.7 1.1 dynamic-slice_bitcast_fusion.2
  65.8 0.1 copy.22
  66.0 0.6 gather_fusion
  66.7 0.4 fusion.23
  67.2 1.1 dynamic-slice_bitcast_fusion.2
  68.5 0.6 gather_fusion
  69.2 0.4 fusion.23
  69.6 1.1 dynamic-slice_bitcast_fusion.2
  70.9 0.6 gather_fusion
  71.6 0.4 fusion.23
  72.1 1.1 dynamic-slice_bitcast_fusion.2
  73.3 0.6 gather_fusion
  74.0 0.4 fusion.23
  74.5 0.1 fusion.9
  74.7 8.6 %all_gather.11 = bf16[1024,256]{1,0:T(8,128)(2,1)S(1)} all-gather(bf16[512,256]{1,0:T(8,128)(2,1)S(1)} %fusion.9), channel_id=1, replica_groups=mesh['row'=4,'replica'=4,'feat'=2] {'feat'}, dimensions={0}, use_global_device_ids=true | all-gather | bytes 786432 | tf_op jit(solution)/shard_map/all_gather | solution.py:40
  83.2 0.4 fusion.13
  83.6 30.5 %all-reduce = (f32[128]{0:T(128)S(1)}, f32[128]{0:T(128)S(1)}) all-reduce(f32[128]{0:T(128)S(1)} %get-tuple-element.166, f32[128]{0:T(128)S(1)} %get-tuple-element.165), channel_id=1, replica_groups=mesh['row'=4,'replica'=4,'feat'=2] {'row','replica'}, use_global_device_ids=true, to_apply=%region_5.6 | all-reduce | flops 256 | bytes 2048 | tf_op jit(solution)/shard_map/psum | solution.py:44
  114.2 0.8 fusion.12
  (47 shorter events, 1.2 us)
Async XLA Ops:
  6.5 76.7 %copy-start = (bf16[256,128]{1,0:T(8,128)(2,1)S(1)}, bf16[256,128]{1,0:T(8,128)(2,1)}, u32[]{:S(2)}) copy-start(bf16[256,128]{1,0:T(8,128)(2,1)} %param.17) | copy-start | bytes 196612
  6.5 58.2 %all-gather.4.cloned.1.call-start = ((), (), s32[]{:S(2)}) async-start(), calls=%async_computation | async-start | bytes 2621440 | tf_op jit(solution)/shard_map/all_gather | solution.py:22
  18.6 1.6 %copy-start.4 = (s32[1,4,4,3]{2,1,3,0:T(4,128)S(1)}, s32[1,4,4,3]{2,1,3,0:T(4,128)}, u32[]{:S(2)}) copy-start(s32[1,4,4,3]{2,1,3,0:T(4,128)} %param.13) | copy-start | bytes 580
  18.6 1.7 %copy-start.5 = (s32[1,4,4]{2,1,0:T(4,128)S(1)}, s32[1,4,4]{2,1,0:T(4,128)}, u32[]{:S(2)}) copy-start(s32[1,4,4]{2,1,0:T(4,128)} %param.14) | copy-start | bytes 196
  18.6 1.8 %copy-start.6 = (s32[1,512]{1,0:T(1,128)S(1)}, s32[1,512]{1,0:T(1,128)}, u32[]{:S(2)}) copy-start(s32[1,512]{1,0:T(1,128)} %param.15) | copy-start | bytes 6148
  18.6 1.8 %copy-start.1 = (bf16[1,1024,256]{2,1,0:T(8,128)(2,1)S(1)}, bf16[1,1024,256]{2,1,0:T(8,128)(2,1)}, u32[]{:S(2)}) copy-start(bf16[1,1024,256]{2,1,0:T(8,128)(2,1)} %all-gather) | copy-start | bytes 1572868
  18.7 1.8 %copy-start.3 = (bf16[256,128]{1,0:T(8,128)(2,1)S(1)}, bf16[256,128]{1,0:T(8,128)(2,1)}, u32[]{:S(2)}) copy-start(bf16[256,128]{1,0:T(8,128)(2,1)} %param.16) | copy-start | bytes 196612
  74.5 8.7 %copy-start.2 = (f32[1024,128]{1,0:T(8,128)S(1)}, f32[1024,128]{1,0:T(8,128)}, u32[]{:S(2)}) copy-start(f32[1024,128]{1,0:T(8,128)} %fusion.10) | copy-start | bytes 1572868
  74.5 39.7 %copy-start.7 = (f32[128]{0:T(128)S(1)}, f32[128]{0:T(128)}, u32[]{:S(2)}) copy-start(f32[128]{0:T(128)} %param.19) | copy-start | bytes 1540
  74.5 39.7 %copy-start.8 = (f32[128]{0:T(128)S(1)}, f32[128]{0:T(128)}, u32[]{:S(2)}) copy-start(f32[128]{0:T(128)} %param.18) | copy-start | bytes 1540
Sparse Core Ops, SparseCore 0:
  18.7 45.9 all-gather.3
where the time goes:
time: 122 us
  blocking collectives  51.1 us (42%)
  waiting for transfers between devices  43.2 us (35%)
  between operations  13.5 us (11%)
  local copies, waits for them, and re-layouts  9.28 us (8%)
  matrix products  3.2 us (3%)
  other arithmetic  1.35 us (1%)
    all_gather x1, waiting for transfers between devices, per_device(): piece = lax.all_gather(pair, 'row', axis=0, tiled=True)  43.2 us
    psum x1, blocking collectives, per_device(): lax.psum((jnp.sum(pre, axis=0), jnp.sum(pre * pre, axis=0)), ('row', 'rep...  30.5 us
    all_gather x1, blocking collectives, per_device(): pair = lax.all_gather(local_x, 'feat', axis=0, tiled=True)  12 us
    all_gather x1, blocking collectives, per_device(): agg_pair = lax.all_gather(agg, 'feat', axis=0, tiled=True)  8.55 us
    squeeze x4, local copies, waits for them, and re-layouts, one_shard(): shard = lax.dynamic_index_in_dim(shards, step, 0, keepdims=False)  4.32 us
  transfers between devices with their start and end apart: 1, of which 1 were waited for; matrix products, arithmetic and copies ran while one was open for 2% of the time, Pallas kernels for 0%

commit v1 on v0

v1 whole, which is shorter than its diff:
```python
import functools

import jax
import jax.numpy as jnp
from jax import lax
from jax.experimental import pallas as pl
from jax.experimental.pallas import tpu as pltpu
from jax.sharding import PartitionSpec as P

AXES = ("row", "replica", "feat")
KERNEL_VMEM = 12 * 1024 * 1024


def whole(shape):
    return pl.BlockSpec(shape, lambda *_: (0,) * len(shape))


def place(xs_ref, piece_refs, feat, blocks, block):
    count = len(piece_refs)
    for k, ref in enumerate(piece_refs):
        owner = lax.rem(feat - k + count, count)
        xs_ref[pl.ds(owner * blocks, blocks)] = ref[...].reshape(blocks, block, ref.shape[-1])


def add_shard(acc, tiles_ref, xs_ref, cols_ref, counts_ref, shard, shards):
    row_blocks, _, slots, block, _ = tiles_ref.shape
    out = []
    for b in range(row_blocks):
        used = counts_ref[b, shard]
        left, right = [], []
        for c in range(slots):
            col = cols_ref[c, b, shard]
            tile = tiles_ref[b, 0, c]
            left.append(jnp.where(c < used, tile, jnp.zeros_like(tile)))
            right.append(xs_ref[col])
        part = jnp.dot(
            jnp.concatenate(left, axis=1),
            jnp.concatenate(right, axis=0),
            preferred_element_type=jnp.float32,
        )
        out.append(part if acc is None else acc[b] + part)
    return out


def aggregate_kernel(shards, feats, sources, first, where_ref, cols_ref, counts_ref, *refs):
    refs = list(refs)
    xs_ref = refs.pop()
    acc_out = refs.pop()
    acc_ref = None if first else refs.pop(0)
    row_blocks = acc_out.shape[0]
    acc = None if first else [acc_ref[b] for b in range(row_blocks)]
    feat = where_ref[0]
    for g in range(sources):
        tiles_ref, *pieces = refs[g * (1 + feats):(g + 1) * (1 + feats)]
        block = tiles_ref.shape[-1]
        place(xs_ref.at[g], pieces, feat, xs_ref.shape[1] // feats, block)
        acc = add_shard(acc, tiles_ref, xs_ref.at[g], cols_ref, counts_ref, where_ref[1 + g], shards)
    for b in range(row_blocks):
        acc_out[b] = acc[b]


def finish_kernel(shards, feats, where_ref, cols_ref, counts_ref, acc_ref, tiles_ref, *refs):
    refs = list(refs)
    xs_ref = refs.pop()
    stats_ref = refs.pop()
    pre_refs = refs[-feats:]
    refs = refs[:-feats]
    pieces = refs[:feats]
    own_ref, degrees_ref = refs[feats:feats + 2]
    weights = refs[feats + 2:]
    row_blocks, block = acc_ref.shape[0], acc_ref.shape[1]
    feat = where_ref[0]
    place(xs_ref, pieces, feat, xs_ref.shape[0] // feats, block)
    acc = add_shard([acc_ref[b] for b in range(row_blocks)], tiles_ref, xs_ref, cols_ref, counts_ref, where_ref[1], shards)
    w_self = jnp.concatenate([w[0] for w in weights], axis=1)
    w_neigh = jnp.concatenate([w[1] for w in weights], axis=1)
    width = weights[0].shape[-1]
    total = square = 0.0
    for b in range(row_blocks):
        rows = pl.ds(b * block, block)
        agg = (acc[b] / degrees_ref[rows, :]).astype(jnp.bfloat16)
        pre = jnp.dot(own_ref[rows, :], w_self, preferred_element_type=jnp.float32) + jnp.dot(
            agg, w_neigh, preferred_element_type=jnp.float32
        )
        total += jnp.sum(pre, axis=0, keepdims=True)
        square += jnp.sum(pre * pre, axis=0, keepdims=True)
        for k in range(feats):
            pre_refs[k][rows, :] = pre[:, k * width:(k + 1) * width]
    both = jnp.concatenate([total, square], axis=0)
    for target in range(feats):
        k_here = lax.rem(feat - target + feats, feats)
        chosen = both[:, :width]
        for k in range(1, feats):
            chosen = jnp.where(k_here == k, both[:, k * width:(k + 1) * width], chosen)
        stats_ref[:, target] = jnp.broadcast_to(chosen[None], (stats_ref.shape[0],) + chosen.shape)


def normalize_kernel(total_nodes, feats, where_ref, stats_ref, gamma_ref, beta_ref, *refs):
    out_ref = refs[-1]
    sums = jnp.sum(stats_ref[...], axis=0)
    mean = sums[0:1] / total_nodes
    var = sums[1:2] / total_nodes - mean * mean
    scale = gamma_ref[...] / jnp.sqrt(var + 1e-05)
    rows = refs[0].shape[0]
    for k in range(feats):
        owner = lax.rem(where_ref[0] - k + feats, feats)
        normed = (refs[k][...] - mean) * scale + beta_ref[...]
        out_ref[pl.ds(pl.multiple_of(owner * rows, rows), rows), :] = jnp.maximum(normed, 0.0).astype(out_ref.dtype)


def per_device(shards, feats, replicas, features, tiles, block_cols, block_counts, degrees, w_self, w_neigh, gamma, beta):
    own = features[0]
    local_tiles = tiles[0]
    cols = jnp.transpose(block_cols[0], (2, 0, 1))
    counts = block_counts[0]
    degrees = degrees[0].astype(jnp.float32)[:, None]
    rows, width = own.shape
    row_blocks, _, slots, block, _ = local_tiles.shape
    feat = lax.axis_index("feat")
    row = lax.axis_index("row")
    xor = shards & (shards - 1) == 0

    def to_row(value, k):
        perm = [(i, i ^ k if xor else (i + k) % shards) for i in range(shards)]
        return lax.ppermute(value, "row", perm)

    def to_feat(value, k):
        return lax.ppermute(value, "feat", [(i, (i + k) % feats) for i in range(feats)])

    def source(k):
        return row ^ k if xor else lax.rem(row - k + shards, shards)

    def spread(here):
        return [here] + [to_feat(here, k) for k in range(1, feats)]

    tile_spec = lambda g: pl.BlockSpec(
        (row_blocks, 1, slots, block, block), lambda i, where, cols, counts: (0, where[1 + g], 0, 0, 0)
    )
    acc_shape = (row_blocks, block, width)
    xs_shape = (feats * rows // block, block, width)

    def where_of(ks):
        return jnp.stack([feat] + [source(k) for k in ks]).astype(jnp.int32)

    def aggregate(acc, ks):
        operands = [] if acc is None else [acc]
        specs = [] if acc is None else [whole(acc_shape)]
        for g, k in enumerate(ks):
            operands += [local_tiles] + pieces[k]
            specs += [tile_spec(g)] + [whole((rows, width))] * feats
        return pl.pallas_call(
            functools.partial(aggregate_kernel, shards, feats, len(ks), acc is None),
            out_shape=jax.ShapeDtypeStruct(acc_shape, jnp.float32),
            grid_spec=pltpu.PrefetchScalarGridSpec(
                num_scalar_prefetch=3, grid=(1,), in_specs=specs, out_specs=whole(acc_shape),
                scratch_shapes=[pltpu.VMEM((len(ks),) + xs_shape, own.dtype)],
            ),
            compiler_params=pltpu.CompilerParams(vmem_limit_bytes=KERNEL_VMEM),
            cost_estimate=pl.CostEstimate(
                flops=2 * rows * slots * block * width * len(ks), bytes_accessed=2 * rows * width * 2 * len(ks), transcendentals=0
            ),
        )(places[ks[0]], cols, counts, *operands)

    arrived = [own] + [to_row(own, k) for k in range(1, shards)]
    pieces = [spread(own)]
    weights = spread(jnp.stack([w_self, w_neigh]))
    places = [where_of([k]) for k in range(shards)]
    arrived[1], cols, counts, degrees, places = lax.optimization_barrier((arrived[1], cols, counts, degrees, places))
    pieces.append(spread(arrived[1]))
    acc = aggregate(None, [0])
    if shards > 2:
        arrived[2], acc, weights = lax.optimization_barrier((arrived[2], acc, weights))
    pieces += [spread(here) for here in arrived[2:]]
    for k in range(1, shards - 1):
        acc = aggregate(acc, [k])
    last = shards - 1
    channels = w_self.shape[1]
    groups = shards * replicas
    *pre, stats = pl.pallas_call(
        functools.partial(finish_kernel, shards, feats),
        out_shape=[jax.ShapeDtypeStruct((rows, channels), jnp.float32)] * feats
        + [jax.ShapeDtypeStruct((groups, feats, 2, channels), jnp.float32)],
        grid_spec=pltpu.PrefetchScalarGridSpec(
            num_scalar_prefetch=3,
            grid=(1,),
            in_specs=[whole(acc_shape), tile_spec(0)]
            + [whole((rows, width))] * feats
            + [whole((rows, width)), whole((rows, 1))]
            + [whole((2, width, channels))] * feats,
            out_specs=[whole((rows, channels))] * feats + [whole((groups, feats, 2, channels))],
            scratch_shapes=[pltpu.VMEM(xs_shape, own.dtype)],
        ),
        compiler_params=pltpu.CompilerParams(vmem_limit_bytes=KERNEL_VMEM),
    )(
        places[last], cols, counts, acc, local_tiles, *pieces[last], own,
        degrees, *weights,
    )
    received = [pre[0]] + [to_feat(pre[k], feats - k) for k in range(1, feats)]
    received = [received[0]] + [received[feats - k] for k in range(1, feats)]
    stats = lax.all_to_all(stats.reshape(groups * feats, 2, channels), AXES, 0, 0)
    out = pl.pallas_call(
        functools.partial(normalize_kernel, rows * feats * groups, feats),
        out_shape=jax.ShapeDtypeStruct((rows * feats, channels), jnp.bfloat16),
        grid_spec=pltpu.PrefetchScalarGridSpec(
            num_scalar_prefetch=1,
            grid=(1,),
            in_specs=[whole((groups * feats, 2, channels)), whole((1, channels)), whole((1, channels))]
            + [whole((rows, channels))] * feats,
            out_specs=whole((rows * feats, channels)),
        ),
        compiler_params=pltpu.CompilerParams(vmem_limit_bytes=KERNEL_VMEM),
    )(feat[None].astype(jnp.int32), stats, gamma[None], beta[None], *received)
    return out[None]


def solution(mesh):
    in_specs = (
        P("replica", ("row", "feat"), None),
        P("replica", ("row", "feat"), None, None, None, None),
        P("replica", ("row", "feat"), None, None),
        P("replica", ("row", "feat"), None),
        P("replica", ("row", "feat")),
        P(None, "feat"),
        P(None, "feat"),
        P("feat"),
        P("feat"),
    )
    out_specs = P("replica", "row", "feat")
    body = functools.partial(per_device, mesh.shape["row"], mesh.shape["feat"], mesh.shape["replica"])
    return jax.shard_map(body, mesh=mesh, in_specs=in_specs, out_specs=out_specs, check_vma=False)
```

time: 122 us -> 51.7 us (0.42)
  blocking collectives: 51.1 us -> 10.7 us
  waiting for transfers between devices: 43.2 us -> 11.8 us
  between operations: 13.5 us -> 0.16 us
  starting transfers between devices: 0.01 us -> 12.5 us
  Pallas kernels: 0 us -> 6.99 us
  local copies, waits for them, and re-layouts: 9.28 us -> 5.79 us
  matrix products: 3.2 us -> 0 us
  other arithmetic: 1.35 us -> 3.37 us
    all_gather x1 -> x0, waiting for transfers between devices: 43.2 us -> none  [per_device(): piece = lax.all_gather(pair, 'row', axis=0, tiled=True)]
    psum x1 -> x0, blocking collectives: 30.5 us -> none  [per_device(): lax.psum((jnp.sum(pre, axis=0), jnp.sum(pre * pre, axis=0)), ('row', 'rep...]
    all_gather x2 -> x0, blocking collectives: 20.6 us -> none  [the longest x1 12 us: per_device(): pair = lax.all_gather(local_x, 'feat', axis=0, tiled=True)]
    ppermute x0 -> x9, starting transfers between devices: none -> 12.5 us  [the longest x6 6.64 us: to_feat(): lax.ppermute(value, 'feat', [(i, (i + k) % feats) for i in range(feats)])]
    ppermute x0 -> x9, waiting for transfers between devices: none -> 11.8 us  [the longest x3 7.38 us: to_row(): return lax.ppermute(value, 'row', perm)]
    all_to_all x0 -> x1, blocking collectives: none -> 10.7 us  [per_device(): lax.all_to_all(stats.reshape(groups * feats, 2, channels), AXES, 0, 0)]
    pallas_call x0 -> x5, Pallas kernels: none -> 6.99 us  [the longest x3 4.93 us: aggregate(): pl.pallas_call(functools.partial(aggregate_kernel, shards, feats, len(ks)...]
    squeeze x4 -> x0, local copies, waits for them, and re-layouts: 4.32 us -> none  [one_shard(): shard = lax.dynamic_index_in_dim(shards, step, 0, keepdims=False)]
  transfers between devices with their start and end apart: 1 -> 9, of which waited for: 1 -> 4; matrix products, arithmetic and copies ran while one was open for 2% -> 8% of each run, Pallas kernels for 0% -> 10%
where the time goes in v1:
time: 51.7 us; the launch traced here: 51.3 us
  starting transfers between devices  12.5 us (24%)
  waiting for transfers between devices  11.8 us (23%)
  blocking collectives  10.7 us (21%)
  Pallas kernels  6.99 us (14%)
  local copies, waits for them, and re-layouts  5.79 us (11%)
  other arithmetic  3.37 us (7%)
    all_to_all x1, blocking collectives, per_device(): lax.all_to_all(stats.reshape(groups * feats, 2, channels), AXES, 0, 0)  10.7 us
    ppermute x3, waiting for transfers between devices, to_row(): return lax.ppermute(value, 'row', perm)  7.38 us
    ppermute x6, starting transfers between devices, to_feat(): lax.ppermute(value, 'feat', [(i, (i + k) % feats) for i in range(feats)])  6.64 us
    ppermute x3, starting transfers between devices, to_row(): return lax.ppermute(value, 'row', perm)  5.86 us
    unnamed x28, local copies, waits for them, and re-layouts  4.99 us
    pallas_call x3, Pallas kernels, aggregate(): pl.pallas_call(functools.partial(aggregate_kernel, shards, feats, len(ks)...  4.93 us
    ppermute x6, waiting for transfers between devices, to_feat(): lax.ppermute(value, 'feat', [(i, (i + k) % feats) for i in range(feats)])  4.39 us
    convert_element_type x1, other arithmetic, per_device(): degrees = degrees[0].astype(jnp.float32)[:, None]  1.25 us
  transfers between devices with their start and end apart: 9, of which 4 were waited for; matrix products, arithmetic and copies ran while one was open for 8% of the time, Pallas kernels for 10%

profile of v1, /device:TPU:0, one launch (start us, length us, event | category | flops | bytes accessed | tf_op | source)
XLA Modules:
  0.0 51.3 jit_solution(9444132669639584515)
XLA Ops:
  0.0 3.1 %collective-permute-start = (bf16[512,256]{1,0:T(8,128)(2,1)}, bf16[512,256]{1,0:T(8,128)(2,1)S(1)}, u32[]{:S(2)}, u32[]{:S(2)}) collective-permute-start(bf16[512,256]{1,0:T(8,128)(2,1)} %bitcast.23), channel_id=1, source_target_pairs={{0,8},{8,0},{16,24},{24,16},{1,9},{9,1},{17,25},{25,17},{2,10},{10... | collective-permute-start | bytes 786440 | tf_op jit(solution)/shard_map/ppermute | solution.py:125
  3.1 1.5 %collective-permute-start.2 = (bf16[512,256]{1,0:T(8,128)(2,1)}, bf16[512,256]{1,0:T(8,128)(2,1)S(1)}, u32[]{:S(2)}, u32[]{:S(2)}) collective-permute-start(bf16[512,256]{1,0:T(8,128)(2,1)} %bitcast.24), channel_id=1, source_target_pairs={{0,1},{1,0},{2,3},{3,2},{4,5},{5,4},{6,7},{7,6},{8,9},{9,8},{10,11... | collective-permute-start | bytes 786440 | tf_op jit(solution)/shard_map/ppermute | solution.py:128
  4.5 2.6 %collective-permute-start.1 = (bf16[512,256]{1,0:T(8,128)(2,1)}, bf16[512,256]{1,0:T(8,128)(2,1)S(1)}, u32[]{:S(2)}, u32[]{:S(2)}) collective-permute-start(bf16[512,256]{1,0:T(8,128)(2,1)} %bitcast.25), channel_id=1, source_target_pairs={{0,16},{8,24},{16,0},{24,8},{1,17},{9,25},{17,1},{25,9},{2,18},{10... | collective-permute-start | bytes 786440 | tf_op jit(solution)/shard_map/ppermute | solution.py:125
  7.4 0.9 %pad_maximum_fusion.refs_4_ = bf16[2,256,128]{2,1,0:T(8,128)(2,1)S(1)} fusion(bf16[1,256,128]{2,1,0:T(8,128)(2,1)} %bitcast.40, bf16[1,256,128]{2,1,0:T(8,128)(2,1)} %bitcast.41), kind=kLoop, calls=%fused_computation | loop fusion | flops 65536 | bytes 262144 | tf_op jit(solution)/shard_map/stack | solution.py:166
  8.7 1.3 %convert_bitcast_fusion = f32[512,1]{0,1:T(1,128)} fusion(s32[1,512]{1,0:T(1,128)} %param.13), kind=kLoop, calls=%fused_computation.1 | loop fusion | flops 512 | bytes 4096 | tf_op jit(solution)/shard_map/convert_element_type | solution.py:116
  9.9 0.6 %pad_add_fusion.2 = (s32[2]{0:T(128)}, s32[2]{0:T(128)S(1)}) fusion(s32[1]{0:T(128)} %bitcast.8, s32[1]{0:T(128)} %bitcast.where_ref, s32[1]{0:T(128)} %bitcast.9), kind=kLoop, calls=%fused_computation.4 | loop fusion | flops 4 | bytes 28 | tf_op jit(solution)/shard_map/stack | solution.py:143
  11.1 2.6 %collective-permute-done.refs_2_ = bf16[512,256]{1,0:T(8,128)(2,1)S(1)} collective-permute-done((bf16[512,256]{1,0:T(8,128)(2,1)}, bf16[512,256]{1,0:T(8,128)(2,1)S(1)}, u32[]{:S(2)}, u32[]{:S(2)}) %collective-permute-start) | collective-permute-done | bytes 262176 | tf_op jit(solution)/shard_map/ppermute | solution.py:125
  13.7 2.1 %collective-permute-start.4 = (bf16[512,256]{1,0:T(8,128)(2,1)S(1)}, bf16[512,256]{1,0:T(8,128)(2,1)}, u32[]{:S(2)}, u32[]{:S(2)}) collective-permute-start(bf16[512,256]{1,0:T(8,128)(2,1)S(1)} %collective-permute-done.refs_2_), channel_id=1, source_target_pairs={{0,1},{1,0},{2,3},{3,2},{4,5},{5,4},{6,7},{7,6},{8,9},{9,8},{10,11... | collective-permute-start | bytes 786440 | tf_op jit(solution)/shard_map/ppermute | solution.py:128
  15.8 1.4 %copy-done = bf16[1,4,4,3,128,128]{5,4,3,2,1,0:T(8,128)(2,1)S(1)} copy-done((bf16[1,4,4,3,128,128]{5,4,3,2,1,0:T(8,128)(2,1)S(1)}, bf16[1,4,4,3,128,128]{5,4,3,2,1,0:T(8,128)(2,1)}, u32[]{:S(2)}) %copy-start) | copy-done | bytes 1572888
  17.2 0.9 %copy-done.2 = bf16[1,512,256]{2,1,0:T(8,128)(2,1)S(1)} copy-done((bf16[1,512,256]{2,1,0:T(8,128)(2,1)S(1)}, bf16[1,512,256]{2,1,0:T(8,128)(2,1)}, u32[]{:S(2)}) %copy-start.2) | copy-done | bytes 262168
  18.2 0.7 %copy-done.6 = s32[1,4,4,3]{2,1,3,0:T(4,128)S(1)} copy-done((s32[1,4,4,3]{2,1,3,0:T(4,128)S(1)}, s32[1,4,4,3]{2,1,3,0:T(4,128)}, u32[]{:S(2)}) %copy-start.6) | copy-done | bytes 216
  18.9 0.7 %copy-done.8 = s32[1,4,4]{2,1,0:T(4,128)S(1)} copy-done((s32[1,4,4]{2,1,0:T(4,128)S(1)}, s32[1,4,4]{2,1,0:T(4,128)}, u32[]{:S(2)}) %copy-start.8) | copy-done | bytes 88
  19.6 1.0 %shard_map.91.refs_0_ = f32[4,128,256]{2,1,0:T(8,128)S(1)} custom-call(s32[2]{0:T(128)S(1)} %get-tuple-element.25.where_ref, s32[3,4,4]{2,1,0:T(4,128)S(1)} %bitcast.29, s32[4,4]{1,0:T(4,128)S(1)} %bitcast.34, bf16[4,4,3,128,128]{4,3,2,1,0:T(8,128)(2,1)S(1)} %bitcast.19, bf16[512,256]{1,0:T(8,128)(2,1)S(1)} %bitcast.27, ...), custom_call_target="tpu_custom_call" | custom-call | flops 100663296 | bytes 524288 | tf_op jit(solution)/shard_map/pallas_call | solution.py:151
  20.6 0.6 %copy-done.4 = bf16[2,256,128]{2,1,0:T(8,128)(2,1)} copy-done((bf16[2,256,128]{2,1,0:T(8,128)(2,1)}, bf16[2,256,128]{2,1,0:T(8,128)(2,1)S(1)}, u32[]{:S(2)}) %copy-start.4) | copy-done | bytes 131096
  21.3 4.8 %collective-permute-done.1.refs_2_ = bf16[512,256]{1,0:T(8,128)(2,1)S(1)} collective-permute-done((bf16[512,256]{1,0:T(8,128)(2,1)}, bf16[512,256]{1,0:T(8,128)(2,1)S(1)}, u32[]{:S(2)}, u32[]{:S(2)}) %collective-permute-start.1) | collective-permute-done | bytes 262176 | tf_op jit(solution)/shard_map/ppermute | solution.py:125
  26.6 1.5 %collective-permute-start.7 = (bf16[512,256]{1,0:T(8,128)(2,1)S(1)}, bf16[512,256]{1,0:T(8,128)(2,1)S(1)}, u32[]{:S(2)}, u32[]{:S(2)}) collective-permute-start(bf16[512,256]{1,0:T(8,128)(2,1)S(1)} %collective-permute-done.6.refs_0_), channel_id=1, source_target_pairs={{0,1},{1,0},{2,3},{3,2},{4,5},{5,4},{6,7},{7,6},{8,9},{9,8},{10,11... | collective-permute-start | bytes 786440 | tf_op jit(solution)/shard_map/ppermute | solution.py:128
  28.1 0.8 %copy.10.refs_3_ = f32[512,1]{1,0:T(8,128)S(1)} copy(f32[512,1]{0,1:T(1,128)} %convert_bitcast_fusion) | data formatting | bytes 4096 | tf_op jit(solution)/shard_map/optimization_barrier | solution.py:168
  29.5 2.0 %shard_map.92.refs_0_ = f32[4,128,256]{2,1,0:T(8,128)S(1)} custom-call(s32[2]{0:T(128)S(1)} %copy-done.11, s32[3,4,4]{2,1,0:T(4,128)S(1)} %bitcast.30, s32[4,4]{1,0:T(4,128)S(1)} %bitcast.35, f32[4,128,256]{2,1,0:T(8,128)S(1)} %shard_map.91.refs_0_, bf16[4,4,3,128,128]{4,3,2,1,0:T(8,128)(2,1)S(1)} %bitcast.20, ...), custom_call_target="tpu_custom_call" | custom-call | flops 100663296 | bytes 524288 | tf_op jit(solution)/shard_map/pallas_call | solution.py:151
  31.5 1.0 %collective-permute-done.5.refs_3_ = bf16[512,256]{1,0:T(8,128)(2,1)} collective-permute-done((bf16[512,256]{1,0:T(8,128)(2,1)S(1)}, bf16[512,256]{1,0:T(8,128)(2,1)}, u32[]{:S(2)}, u32[]{:S(2)}) %collective-permute-start.5) | collective-permute-done | bytes 262176 | tf_op jit(solution)/shard_map/ppermute | solution.py:128
  32.5 2.0 %shard_map.93.acc_ref = f32[4,128,256]{2,1,0:T(8,128)S(1)} custom-call(s32[2]{0:T(128)S(1)} %copy-done.10, s32[3,4,4]{2,1,0:T(4,128)S(1)} %bitcast.31, s32[4,4]{1,0:T(4,128)S(1)} %bitcast.36, f32[4,128,256]{2,1,0:T(8,128)S(1)} %shard_map.92.refs_0_, bf16[4,4,3,128,128]{4,3,2,1,0:T(8,128)(2,1)S(1)} %bitcast.21, ...), custom_call_target="tpu_custom_call" | custom-call | flops 100663296 | bytes 524288 | tf_op jit(solution)/shard_map/pallas_call | solution.py:151
  34.5 3.4 %collective-permute-done.7.refs_1_ = bf16[512,256]{1,0:T(8,128)(2,1)S(1)} collective-permute-done((bf16[512,256]{1,0:T(8,128)(2,1)S(1)}, bf16[512,256]{1,0:T(8,128)(2,1)S(1)}, u32[]{:S(2)}, u32[]{:S(2)}) %collective-permute-start.7) | collective-permute-done | bytes 262176 | tf_op jit(solution)/shard_map/ppermute | solution.py:128
  37.9 1.2 %shard_map.94 = (f32[512,128]{1,0:T(8,128)S(1)}, f32[512,128]{1,0:T(8,128)S(1)}, f32[16,2,2,128]{3,2,1,0:T(2,128)S(1)}) custom-call(s32[2]{0:T(128)S(1)} %get-tuple-element.20.where_ref, s32[3,4,4]{2,1,0:T(4,128)S(1)} %bitcast.32, s32[4,4]{1,0:T(4,128)S(1)} %bitcast.37, f32[4,128,256]{2,1,0:T(8,128)S(1)} %shard_map.93.acc_ref, ...), custom_call_target="tpu_custom_call" | custom-call | tf_op jit(solution)/shard_map/pallas_call | solution.py:179
  39.7 10.7 %all_to_all.5.stats_ref = f32[32,2,128]{2,1,0:T(2,128)S(1)} all-to-all(f32[32,2,128]{2,1,0:T(2,128)S(1)} %bitcast.33), channel_id=1, replica_groups=mesh['row'=4,'replica'=4,'feat'=2] {'row','replica','feat'}, dimensions={0} | all-to-all | bytes 65536 | tf_op jit(solution)/shard_map/all_to_all | solution.py:200
  50.5 0.8 %shard_map.95 = bf16[1024,128]{1,0:T(8,128)(2,1)} custom-call(s32[1]{0:T(128)} %bitcast.where_ref, f32[32,2,128]{2,1,0:T(2,128)S(1)} %all_to_all.5.stats_ref, f32[1,128]{1,0:T(1,128)S(1)} %bitcast.38, f32[1,128]{1,0:T(1,128)S(1)} %bitcast.39, f32[512,128]{1,0:T(8,128)S(1)} %get-tuple-element.33.refs_0_, f32[512,128]{1,0:T(8,128)S(1)} %collective-permute-done.8.refs_1_), custom_call_target="tpu_custom_call" | custom-call | tf_op jit(solution)/shard_map/pallas_call | solution.py:201
  (33 shorter events, 2.9 us)
Async XLA Ops:
  0.0 13.7 %collective-permute-start = (bf16[512,256]{1,0:T(8,128)(2,1)}, bf16[512,256]{1,0:T(8,128)(2,1)S(1)}, u32[]{:S(2)}, u32[]{:S(2)}) collective-permute-start(bf16[512,256]{1,0:T(8,128)(2,1)} %bitcast.23), channel_id=1, source_target_pairs={{0,8},{8,0},{16,24},{24,16},{1,9},{9,1},{17,25},{25,17},{2,10},{10... | collective-permute-start | bytes 786440 | tf_op jit(solution)/shard_map/ppermute | solution.py:125
  3.1 12.8 %collective-permute-start.2 = (bf16[512,256]{1,0:T(8,128)(2,1)}, bf16[512,256]{1,0:T(8,128)(2,1)S(1)}, u32[]{:S(2)}, u32[]{:S(2)}) collective-permute-start(bf16[512,256]{1,0:T(8,128)(2,1)} %bitcast.24), channel_id=1, source_target_pairs={{0,1},{1,0},{2,3},{3,2},{4,5},{5,4},{6,7},{7,6},{8,9},{9,8},{10,11... | collective-permute-start | bytes 786440 | tf_op jit(solution)/shard_map/ppermute | solution.py:128
  4.5 21.5 %collective-permute-start.1 = (bf16[512,256]{1,0:T(8,128)(2,1)}, bf16[512,256]{1,0:T(8,128)(2,1)S(1)}, u32[]{:S(2)}, u32[]{:S(2)}) collective-permute-start(bf16[512,256]{1,0:T(8,128)(2,1)} %bitcast.25), channel_id=1, source_target_pairs={{0,16},{8,24},{16,0},{24,8},{1,17},{9,25},{17,1},{25,9},{2,18},{10... | collective-permute-start | bytes 786440 | tf_op jit(solution)/shard_map/ppermute | solution.py:125
  7.1 19.5 %collective-permute-start.6 = (bf16[512,256]{1,0:T(8,128)(2,1)}, bf16[512,256]{1,0:T(8,128)(2,1)S(1)}, u32[]{:S(2)}, u32[]{:S(2)}) collective-permute-start(bf16[512,256]{1,0:T(8,128)(2,1)} %bitcast.26), channel_id=1, source_target_pairs={{0,24},{8,16},{16,8},{24,0},{1,25},{9,17},{17,9},{25,1},{2,26},{10... | collective-permute-start | bytes 786440 | tf_op jit(solution)/shard_map/ppermute | solution.py:125
  7.4 21.6 %copy-start.7 = (s32[1,4,4,3]{2,1,3,0:T(4,128)S(1)}, s32[1,4,4,3]{2,1,3,0:T(4,128)}, u32[]{:S(2)}) copy-start(s32[1,4,4,3]{2,1,3,0:T(4,128)} %param.11) | copy-start | bytes 580
  7.4 21.6 %copy-start.9 = (s32[1,4,4]{2,1,0:T(4,128)S(1)}, s32[1,4,4]{2,1,0:T(4,128)}, u32[]{:S(2)}) copy-start(s32[1,4,4]{2,1,0:T(4,128)} %param.12) | copy-start | bytes 196
  8.3 12.3 %collective-permute-start.3 = (bf16[2,256,128]{2,1,0:T(8,128)(2,1)S(1)}, bf16[2,256,128]{2,1,0:T(8,128)(2,1)S(1)}, u32[]{:S(2)}, u32[]{:S(2)}) collective-permute-start(bf16[2,256,128]{2,1,0:T(8,128)(2,1)S(1)} %pad_maximum_fusion.refs_4_), channel_id=1, source_target_pairs={{0,1},{1,0},{2,3},{3,2},{4,5},{5,4},{6,7},{7,6},{8,9},{9,8},{10,11... | collective-permute-start | bytes 393224 | tf_op jit(solution)/shard_map/ppermute | solution.py:128
  13.7 15.2 %collective-permute-start.4 = (bf16[512,256]{1,0:T(8,128)(2,1)S(1)}, bf16[512,256]{1,0:T(8,128)(2,1)}, u32[]{:S(2)}, u32[]{:S(2)}) collective-permute-start(bf16[512,256]{1,0:T(8,128)(2,1)S(1)} %collective-permute-done.refs_2_), channel_id=1, source_target_pairs={{0,1},{1,0},{2,3},{3,2},{4,5},{5,4},{6,7},{7,6},{8,9},{9,8},{10,11... | collective-permute-start | bytes 786440 | tf_op jit(solution)/shard_map/ppermute | solution.py:128
  15.8 1.4 %copy-start = (bf16[1,4,4,3,128,128]{5,4,3,2,1,0:T(8,128)(2,1)S(1)}, bf16[1,4,4,3,128,128]{5,4,3,2,1,0:T(8,128)(2,1)}, u32[]{:S(2)}) copy-start(bf16[1,4,4,3,128,128]{5,4,3,2,1,0:T(8,128)(2,1)} %param.10) | copy-start | bytes 4718596
  17.2 0.9 %copy-start.2 = (bf16[1,512,256]{2,1,0:T(8,128)(2,1)S(1)}, bf16[1,512,256]{2,1,0:T(8,128)(2,1)}, u32[]{:S(2)}) copy-start(bf16[1,512,256]{2,1,0:T(8,128)(2,1)} %param.9) | copy-start | bytes 786436
  18.2 0.7 %copy-start.6 = (s32[1,4,4,3]{2,1,3,0:T(4,128)S(1)}, s32[1,4,4,3]{2,1,3,0:T(4,128)}, u32[]{:S(2)}) copy-start(s32[1,4,4,3]{2,1,3,0:T(4,128)} %param.11) | copy-start | bytes 580
  18.9 0.7 %copy-start.8 = (s32[1,4,4]{2,1,0:T(4,128)S(1)}, s32[1,4,4]{2,1,0:T(4,128)}, u32[]{:S(2)}) copy-start(s32[1,4,4]{2,1,0:T(4,128)} %param.12) | copy-start | bytes 196
  19.6 9.4 %copy-start.1 = (bf16[1,4,4,3,128,128]{5,4,3,2,1,0:T(8,128)(2,1)S(1)}, bf16[1,4,4,3,128,128]{5,4,3,2,1,0:T(8,128)(2,1)}, u32[]{:S(2)}) copy-start(bf16[1,4,4,3,128,128]{5,4,3,2,1,0:T(8,128)(2,1)} %param.10) | copy-start | bytes 4718596
  20.6 0.7 %copy-start.4 = (bf16[2,256,128]{2,1,0:T(8,128)(2,1)}, bf16[2,256,128]{2,1,0:T(8,128)(2,1)S(1)}, u32[]{:S(2)}) copy-start(bf16[2,256,128]{2,1,0:T(8,128)(2,1)S(1)} %collective-permute-done.3.refs_5_) | copy-start | bytes 393220
  26.1 6.5 %collective-permute-start.5 = (bf16[512,256]{1,0:T(8,128)(2,1)S(1)}, bf16[512,256]{1,0:T(8,128)(2,1)}, u32[]{:S(2)}, u32[]{:S(2)}) collective-permute-start(bf16[512,256]{1,0:T(8,128)(2,1)S(1)} %collective-permute-done.1.refs_2_), channel_id=1, source_target_pairs={{0,1},{1,0},{2,3},{3,2},{4,5},{5,4},{6,7},{7,6},{8,9},{9,8},{10,11... | collective-permute-start | bytes 786440 | tf_op jit(solution)/shard_map/ppermute | solution.py:128
  26.6 11.3 %collective-permute-start.7 = (bf16[512,256]{1,0:T(8,128)(2,1)S(1)}, bf16[512,256]{1,0:T(8,128)(2,1)S(1)}, u32[]{:S(2)}, u32[]{:S(2)}) collective-permute-start(bf16[512,256]{1,0:T(8,128)(2,1)S(1)} %collective-permute-done.6.refs_0_), channel_id=1, source_target_pairs={{0,1},{1,0},{2,3},{3,2},{4,5},{5,4},{6,7},{7,6},{8,9},{9,8},{10,11... | collective-permute-start | bytes 786440 | tf_op jit(solution)/shard_map/ppermute | solution.py:128
  28.9 3.6 %copy-start.10 = (s32[2]{0:T(128)S(1)}, s32[2]{0:T(128)}, u32[]{:S(2)}) copy-start(s32[2]{0:T(128)} %get-tuple-element.23.where_ref) | copy-start | bytes 28
  29.0 0.6 %copy-start.11 = (s32[2]{0:T(128)S(1)}, s32[2]{0:T(128)}, u32[]{:S(2)}) copy-start(s32[2]{0:T(128)} %get-tuple-element.24.where_ref) | copy-start | bytes 28
  31.5 6.4 %copy-start.3 = (bf16[1,512,256]{2,1,0:T(8,128)(2,1)S(1)}, bf16[1,512,256]{2,1,0:T(8,128)(2,1)}, u32[]{:S(2)}) copy-start(bf16[1,512,256]{2,1,0:T(8,128)(2,1)} %param.9) | copy-start | bytes 786436
  31.5 6.4 %copy-start.5 = (bf16[2,256,128]{2,1,0:T(8,128)(2,1)S(1)}, bf16[2,256,128]{2,1,0:T(8,128)(2,1)}, u32[]{:S(2)}) copy-start(bf16[2,256,128]{2,1,0:T(8,128)(2,1)} %copy-done.4) | copy-start | bytes 393220
  34.5 16.0 %copy-start.12 = (f32[128]{0:T(128)S(1)}, f32[128]{0:T(128)}, u32[]{:S(2)}) copy-start(f32[128]{0:T(128)} %param.16) | copy-start | bytes 1540
  34.5 15.9 %copy-start.13 = (f32[128]{0:T(128)S(1)}, f32[128]{0:T(128)}, u32[]{:S(2)}) copy-start(f32[128]{0:T(128)} %param.17) | copy-start | bytes 1540
  39.1 11.3 %collective-permute-start.8 = (f32[512,128]{1,0:T(8,128)S(1)}, f32[512,128]{1,0:T(8,128)S(1)}, u32[]{:S(2)}, u32[]{:S(2)}) collective-permute-start(f32[512,128]{1,0:T(8,128)S(1)} %get-tuple-element.34), channel_id=1, source_target_pairs={{0,1},{1,0},{2,3},{3,2},{4,5},{5,4},{6,7},{7,6},{8,9},{9,8},{10,11... | collective-permute-start | bytes 786440 | tf_op jit(solution)/shard_map/ppermute | solution.py:128
